TPU v7x, 128 devices: a whole 4x4x4 slice. The times are simulated.
128 devices in a mesh: group: 4 (over x), shard: 32 (over z, y, core).
Axes of the slice: x: 4, y: 4, z: 4, core: 2. Of those that a mesh axis runs over, the one named last changes fastest.
Arguments:
- samples: bfloat16 [16384, 1, 4096], P(('group', 'shard')), may hold values from -6 to 6
- fan_taps: float32 [33, 2048], replicated, may hold values from -1 to 1
- pair_blocks: int32 [512, 2], replicated, may hold values from 0 to 127
- pair_valid: int32 [512], P(('group', 'shard')), may hold values 0 or 1
- coil_offsets: int32 [128], replicated, may hold values from 0 to 63
Outputs:
- correlations: float32 [512, 128, 512], P(('group', 'shard'))
Inputs may be any that keep to these rules, and one draw needn't show every extreme that they name: `pair_blocks`: block indices.
All inputs are finite; a program needn't handle non-finite values. No bound on the sum of `pair_valid` on one device may be relied on, other than what follows from the above.
Results may differ from a plain program's by a relative error of at most 0.0076.
Values may be sent and summed in bfloat16 or wider, within the bound.
A program may use at most 192 MiB of HBM per device.

v0:
```python
import jax
import jax.numpy as jnp
from jax import lax
from jax.sharding import PartitionSpec as P

HALF = 16
SMOOTH = 64
NLAG = 512
EPSILON = 1e-05


def with_halo(cells, sides, width):
    for axis, dim in sides:
        count = lax.axis_size(axis)
        ends = count - 1
        head = lax.slice_in_dim(cells, 0, width, axis=dim)
        tail = lax.slice_in_dim(cells, cells.shape[dim] - width, cells.shape[dim], axis=dim)
        cells = jnp.concatenate(
            [
                lax.ppermute(tail, axis, [(i, (i + 1) % count) for i in range(ends)]),
                cells,
                lax.ppermute(head, axis, [((i + 1) % count, i) for i in range(ends)]),
            ],
            axis=dim,
        )
    return cells


def forward_tables(length, bin_count):
    split = 1 << length.bit_length() // 2
    coarse_n = (jnp.arange(length // split, dtype=jnp.int32) * split)[:, None]
    fine_n = jnp.arange(split, dtype=jnp.int32)[:, None]
    cols_k = jnp.arange(bin_count, dtype=jnp.int32)[None, :]
    coarse_ph = jnp.mod(coarse_n * cols_k, length).astype(jnp.float32) * (2.0 * jnp.pi / length)
    fine_ph = jnp.mod(fine_n * cols_k, length).astype(jnp.float32) * (2.0 * jnp.pi / length)
    cos_a = jnp.cos(coarse_ph)[:, None, :]
    sin_a = jnp.sin(coarse_ph)[:, None, :]
    cos_b = jnp.cos(fine_ph)[None, :, :]
    sin_b = jnp.sin(fine_ph)[None, :, :]
    cosine = (cos_a * cos_b - sin_a * sin_b).reshape(length, bin_count)
    sine_vals = (sin_a * cos_b + cos_a * sin_b).reshape(length, bin_count)
    scaled = 1.0 / jnp.sqrt(jnp.float32(length))
    return (jnp.concatenate([cosine, -sine_vals], axis=1) * scaled).astype(jnp.bfloat16)


def inverse_tables(length, bin_count, lag_count):
    freq_index = jnp.arange(bin_count, dtype=jnp.int32)[:, None]
    lagged = jnp.arange(lag_count, dtype=jnp.int32)[None, :] - lag_count // 2
    phases = jnp.mod(freq_index * lagged, length).astype(jnp.float32) * (2.0 * jnp.pi / length)
    return jnp.stack([jnp.cos(phases), -jnp.sin(phases)]).astype(jnp.bfloat16)


def box_mean(power_sum):
    bin_count = power_sum.shape[1]
    zero_row = jnp.zeros_like(power_sum[:, :1])
    prefix = jnp.concatenate([zero_row, jnp.cumsum(power_sum, axis=1)], axis=1)
    last_row = prefix[:, bin_count : bin_count + 1]
    first_row = prefix[:, 0:1]
    upper_vals = jnp.concatenate(
        [
            prefix[:, SMOOTH + 1 :],
            jnp.broadcast_to(last_row, (prefix.shape[0], SMOOTH) + prefix.shape[2:]),
        ],
        axis=1,
    )
    lower_vals = jnp.concatenate(
        [
            jnp.broadcast_to(first_row, (prefix.shape[0], SMOOTH + 1) + prefix.shape[2:]),
            prefix[:, 1 : bin_count - SMOOTH],
        ],
        axis=1,
    )
    bins_k = jnp.arange(bin_count, dtype=jnp.int32)
    counts = (
        jnp.minimum(bins_k + SMOOTH, bin_count - 1) - jnp.maximum(bins_k - SMOOTH, 0) + 1
    ).astype(jnp.float32)
    return (upper_vals - lower_vals) / counts[None, :, None]


def whiten(padded, fan_taps):
    width = padded.shape[3] - 2 * HALF
    filtered = jnp.zeros(padded.shape[:3] + (width,), jnp.float32)
    for offset in range(2 * HALF + 1):
        filtered = filtered + fan_taps[offset][None, None, :, None] * padded[
            :, :, :, offset : offset + width
        ].astype(jnp.float32)
    power_sum = filtered[:, 0] * filtered[:, 0] + filtered[:, 1] * filtered[:, 1]
    mean_power = box_mean(power_sum)
    return (filtered * lax.rsqrt(mean_power + EPSILON)[:, None]).astype(jnp.bfloat16)


def body(samples, fan_taps, pair_blocks, pair_valid, coil_offsets):
    block_width = samples.shape[0]
    segments = samples.shape[1]
    length = samples.shape[2]
    bin_count = length // 2
    groups = lax.axis_size("group")
    shards = lax.axis_size("shard")
    devices = groups * shards
    bins_device = bin_count // devices
    forward = forward_tables(length, bin_count)
    spectra = jnp.einsum("cst,tk->skc", samples, forward, preferred_element_type=jnp.float32)
    padded = with_halo(
        spectra.astype(jnp.bfloat16).reshape(segments, 2, bin_count, samples.shape[0]),
        ((("group", "shard"), 3),),
        HALF,
    )
    whitened = whiten(padded, fan_taps)
    banded = lax.all_to_all(whitened, ("group", "shard"), split_axis=2, concat_axis=3, tiled=True)
    first_block = pair_blocks[:, 0]
    second_block = pair_blocks[:, 1]
    blocks = banded.reshape(segments, 2, bins_device, devices, block_width)
    rolled = jnp.roll(blocks, -(block_width // 2), axis=4)
    left_side = jnp.take(blocks, first_block, axis=3)
    right_side = jnp.take(rolled, second_block, axis=3)
    form = "skpc,skpc->kpc"
    real_part = jnp.einsum(
        form, left_side[:, 0], right_side[:, 0], preferred_element_type=jnp.float32
    ) + jnp.einsum(form, left_side[:, 1], right_side[:, 1], preferred_element_type=jnp.float32)
    imag_part = jnp.einsum(
        form, left_side[:, 1], right_side[:, 0], preferred_element_type=jnp.float32
    ) - jnp.einsum(form, left_side[:, 0], right_side[:, 1], preferred_element_type=jnp.float32)
    block_ids = jnp.arange(devices, dtype=jnp.int32)[None, :]
    first_offset = jnp.sum(
        jnp.where(first_block[:, None] == block_ids, coil_offsets[None, :], 0), axis=1
    )
    second_offset = jnp.sum(
        jnp.where(second_block[:, None] == block_ids, coil_offsets[None, :], 0), axis=1
    )
    shift_samples = first_offset - second_offset
    bin_index = lax.axis_index(("group", "shard")) * bins_device + jnp.arange(
        bins_device, dtype=jnp.int32
    )
    phases = jnp.mod(bin_index[:, None] * shift_samples[None, :], length).astype(jnp.float32) * (
        2.0 * jnp.pi / length
    )
    cosine = jnp.cos(phases)[:, :, None]
    sine_values = jnp.sin(phases)[:, :, None]
    cross_spec = jnp.stack(
        [real_part * cosine + imag_part * sine_values, imag_part * cosine - real_part * sine_values]
    ).astype(jnp.bfloat16)
    owned_spec = lax.all_to_all(
        cross_spec, ("group", "shard"), split_axis=2, concat_axis=1, tiled=True
    )
    inverse = inverse_tables(length, bin_count, NLAG)
    correlations = jnp.einsum(
        "rkpc,rkl->pcl", owned_spec, inverse, preferred_element_type=jnp.float32
    )
    weights = pair_valid.astype(jnp.float32) / jnp.sqrt(jnp.float32(bin_count * segments))
    return correlations * weights[:, None, None]


def solution(mesh):
    return jax.shard_map(
        body,
        mesh=mesh,
        in_specs=(P(("group", "shard"), None, None), P(), P(), P(("group", "shard")), P()),
        out_specs=P(("group", "shard"), None, None),
        check_vma=False,
    )
```

profile of v0, /device:TPU:1, one launch (start us, length us, event | category | flops | bytes accessed | tf_op | source)
XLA Modules:
  0.0 236.7 jit_solution(15228262035999444965)
XLA Ops:
  0.0 2.0 fusion.74
  2.1 2.1 fusion.77
  4.2 22.0 %multiply_subtract_fusion = (f32[64,64,2048]{2,1,0:T(8,128)}, f32[64,64,2048]{2,1,0:T(8,128)}) fusion(f32[64,2048]{1,0:T(8,128)S(1)} %get-tuple-element.57, f32[64,2048]{1,0:T(8,128)S(1)} %get-tuple-element.56, f32[64,2048]{1,0:T(8,128)S(1)} %get-tuple-element.58, f32[64,2048]{1,0:T(8,128)S(1)} %get-tuple-element.55), kind=kLoop, calls=%fused_computation.5 | loop fusion | flops 58720256 | bytes 69206016 | tf_op jit(solution)/shard_map/sub | solution.py:40
  26.2 22.9 %fusion.3 = bf16[4096,128]{1,0:T(8,128)(2,1)S(1)} fusion(f32[4096,2048]{1,0:T(8,128)} %bitcast.155, f32[4096,2048]{1,0:T(8,128)} %bitcast.154, bf16[128,1,4096]{2,0,1:T(8,128)(2,1)S(1)} %copy-done), kind=kOutput, calls=%fused_computation.76 | convolution fusion | flops 4345823232 | bytes 69206016 | tf_op jit(solution)/shard_map/cst,tk->skc/dot_general | solution.py:102
  49.5 0.6 copy-done.3
  50.4 4.6 %collective-permute-start = (bf16[1,2,2048,16]{2,3,1,0:T(8,128)(2,1)S(1)}, bf16[1,2,2048,16]{2,3,1,0:T(8,128)(2,1)S(1)}, u32[]{:S(2)}, u32[]{:S(2)}) collective-permute-start(bf16[1,2,2048,16]{2,3,1,0:T(8,128)(2,1)S(1)} %copy.61), channel_id=1, source_target_pairs={{0,1},{1,2},{2,3},{3,4},{4,5},{5,6},{6,7},{7,8},{8,9},{9,10},{10,1... | collective-permute-start | bytes 393224 | tf_op jit(solution)/shard_map/ppermute | solution.py:20
  55.3 2.2 collective-permute-start.1
  57.6 0.7 fusion.93
  58.3 0.7 fusion.94
  60.1 0.9 copy.75
  60.9 0.6 fusion.86
  61.5 1.3 copy.62
  62.9 1.3 copy.64
  64.3 40.0 %multiply_add_fusion = f32[1,2,2048,128]{3,2,1,0:T(8,128)S(1)} fusion(bf16[1,2,2048,128]{3,2,1,0:T(8,128)(2,1)S(1)} %bitcast.157, bf16[1,2,2048,16]{3,2,1,0:T(8,128)(2,1)} %copy.64, bf16[1,2,2048,16]{3,2,1,0:T(8,128)(2,1)} %copy.62, f32[2048]{0:T(1024)} %bitcast.194, f32[2048]{0:T(1024)} %bitcast.195, f32[2048]{0:T(1024)S(1)} %bitcast.164, ...), kind=kLoop, calls=%fused_computation.103 | loop fusion | flops 101711872 | bytes 3678208 | tf_op jit(solution)/shard_map/add | solution.py:84
  104.3 0.6 fusion.60
  105.0 1.3 copy.66
  106.3 1.3 bitcast_add_fusion
  108.9 9.5 %copy.67 = bf16[1,2,2048,128]{3,1,0,2:T(2,128)(2,1)} copy(bf16[1,2,2048,128]{3,2,1,0:T(8,128)(2,1)S(1)} %multiply_convert_fusion) | data formatting | bytes 2097152 | tf_op jit(solution)/shard_map/convert_element_type | solution.py:89
  118.3 11.2 %all-to-all-start = ((bf16[1,2,2048,128]{3,1,0,2:T(2,128)(2,1)}), bf16[1,2,2048,128]{3,1,0,2:T(2,128)(2,1)S(1)}, u32[]{:S(2)}, u32[]{:S(2)}) async-start(bf16[1,2,2048,128]{3,1,0,2:T(2,128)(2,1)} %copy.67), calls=%async_computation | async-start | bytes 2097152 | tf_op jit(solution)/shard_map/all_to_all | solution.py:109
  129.6 19.0 %all-to-all-done = bf16[1,2,2048,128]{3,1,0,2:T(2,128)(2,1)S(1)} async-done(((bf16[1,2,2048,128]{3,1,0,2:T(2,128)(2,1)}), bf16[1,2,2048,128]{3,1,0,2:T(2,128)(2,1)S(1)}, u32[]{:S(2)}, u32[]{:S(2)}) %all-to-all-start) | async-done | bytes 1048608 | tf_op jit(solution)/shard_map/all_to_all | solution.py:109
  149.2 0.6 maximum_bitcast_fusion.6
  149.8 3.5 %gather_fusion.1 = bf16[512,2,16,128]{3,2,1,0:T(8,128)(2,1)} fusion(bf16[2,16,128,128]{3,1,2,0:T(8,128)(2,1)S(1)} %maximum_bitcast_fusion.6, s32[1024]{0:T(1024)S(1)} %pad_clamp_fusion), kind=kCustom, calls=%fused_computation.1.clone | custom fusion | bytes 8390656 | tf_op jit(solution)/shard_map/jit(_take)/gather | solution.py:115
  153.3 4.6 %bitcast_select_fusion = bf16[1,2,16,512,128]{4,2,3,1,0:T(8,128)(2,1)} fusion(bf16[512,2,16,128]{3,2,1,0:T(8,128)(2,1)} %gather_fusion.1, pred[512]{0:T(512)(128)(4,1)S(1)} %compare_and_fusion), kind=kLoop, calls=%fused_computation.90 | loop fusion | flops 2097152 | bytes 8389120 | tf_op jit(solution)/shard_map/jit(_take)/select_n | solution.py:115
  157.9 3.5 %gather_fusion = bf16[512,2,16,128]{3,2,1,0:T(8,128)(2,1)} fusion(bf16[2,16,128,128]{3,1,2,0:T(8,128)(2,1)S(1)} %bitcast.153, s32[1024]{0:T(1024)S(1)} %pad_clamp_fusion.1), kind=kCustom, calls=%fused_computation.clone | custom fusion | bytes 8390656 | tf_op jit(solution)/shard_map/jit(_take)/gather | solution.py:114
  161.4 3.4 %bitcast_select_fusion.1 = bf16[1,2,16,512,128]{4,2,1,3,0:T(8,128)(2,1)S(1)} fusion(bf16[512,2,16,128]{3,2,1,0:T(8,128)(2,1)} %gather_fusion, pred[512]{0:T(512)(128)(4,1)S(1)} %compare_and_fusion.1), kind=kLoop, calls=%fused_computation.91 | loop fusion | flops 2097152 | bytes 8389120 | tf_op jit(solution)/shard_map/jit(_take)/select_n | solution.py:114
  164.9 3.6 %fusion.20 = (bf16[1,16,512,128]{3,1,2,0:T(8,128)(2,1)S(1)}, bf16[1,16,512,128]{3,1,2,0:T(8,128)(2,1)S(1)}) fusion(f32[16,512]{0,1:T(8,128)S(1)} %copy-done.6, f32[16,512]{0,1:T(8,128)S(1)} %copy.72, bf16[1,2,16,512,128]{4,2,3,1,0:T(8,128)(2,1)S(1)} %copy-done.2, bf16[1,2,16,512,128]{4,2,1,3,0:T(8,128)(2,1)S(1)} %bitcast_select_fusion.1), kind=kLoop, calls=%fused_computation.99 | loop fusion | flops 18874368 | bytes 12648448 | tf_op jit(solution)/shard_map/stack | solution.py:139
  168.9 2.7 %copy.76 = bf16[2,16,512,128]{3,1,0,2:T(8,128)(2,1)} copy(bf16[2,16,512,128]{3,1,2,0:T(8,128)(2,1)S(1)} %pad_maximum_fusion) | data formatting | bytes 8388608 | tf_op jit(solution)/shard_map/stack | solution.py:139
  171.7 5.8 %all-to-all-start.1 = ((bf16[2,16,512,128]{3,1,0,2:T(8,128)(2,1)}), bf16[2,16,512,128]{3,1,0,2:T(8,128)(2,1)}, u32[]{:S(2)}, u32[]{:S(2)}) async-start(bf16[2,16,512,128]{3,1,0,2:T(8,128)(2,1)} %copy.76), calls=%async_computation.1 | async-start | bytes 8388608 | tf_op jit(solution)/shard_map/all_to_all | solution.py:142
  177.5 18.2 %cosine_convert_fusion = (bf16[1,2048,512]{2,1,0:T(8,128)(2,1)S(1)}, bf16[1,2048,512]{2,1,0:T(8,128)(2,1)}) fusion(s32[512]{0:T(512)S(1)} %iota_add_fusion.2), kind=kLoop, calls=%fused_computation.93 | loop fusion | flops 17825792 | bytes 4196352 | tf_op jit(solution)/shard_map/convert.12
  195.7 34.5 %all-to-all-done.1 = bf16[2,16,512,128]{3,1,0,2:T(8,128)(2,1)} async-done(((bf16[2,16,512,128]{3,1,0,2:T(8,128)(2,1)}), bf16[2,16,512,128]{3,1,0,2:T(8,128)(2,1)}, u32[]{:S(2)}, u32[]{:S(2)}) %all-to-all-start.1) | async-done | bytes 4194336 | tf_op jit(solution)/shard_map/all_to_all | solution.py:142
  230.2 3.1 %copy.78 = bf16[2,128,16,4,128]{4,2,1,3,0:T(8,128)(2,1)S(1)} copy(bf16[2,128,16,4,128]{4,2,0,3,1:T(8,128)(2,1)} %bitcast.67) | data formatting | bytes 8388608 | tf_op jit(solution)/shard_map/all_to_all | solution.py:142
  233.3 3.3 %fusion.23 = f32[4,128,512]{2,1,0:T(8,128)} fusion(bf16[2,2048,4,128]{3,1,2,0:T(8,128)(2,1)S(1)} %bitcast.162, bf16[1,2048,512]{2,1,0:T(8,128)(2,1)S(1)} %copy-done.5, bf16[1,2048,512]{2,1,0:T(8,128)(2,1)S(1)} %get-tuple-element.53, f32[4]{0:T(128)S(1)} %convert_multiply_fusion.4), kind=kOutput, calls=%fused_computation.105 | convolution fusion | flops 2149842944 | bytes 9437200 | tf_op jit(solution)/shard_map/rkpc,rkl->pcl/dot_general | solution.py:146
  (80 shorter events, 4.4 us)
Async XLA Ops:
  0.0 26.2 %copy-start = (bf16[128,1,4096]{2,0,1:T(8,128)(2,1)S(1)}, bf16[128,1,4096]{2,0,1:T(8,128)(2,1)}, u32[]{:S(2)}) copy-start(bf16[128,1,4096]{2,0,1:T(8,128)(2,1)} %param.7) | copy-start | bytes 3145732
  49.1 1.0 copy-start.3
  50.1 7.5 %copy-start.7 = (f32[33,2048]{1,0:T(8,128)S(1)}, f32[33,2048]{1,0:T(8,128)}, u32[]{:S(2)}) copy-start(f32[33,2048]{1,0:T(8,128)} %param.8) | copy-start | bytes 811012
  50.1 9.0 %copy-start.21 = (s32[512,2]{0,1:T(2,128)S(1)}, s32[512,2]{0,1:T(2,128)}, u32[]{:S(2)}) copy-start(s32[512,2]{0,1:T(2,128)} %param.9) | copy-start | bytes 12292
  50.1 9.0 %copy-start.22 = (s32[128]{0:T(128)S(1)}, s32[128]{0:T(128)}, u32[]{:S(2)}) copy-start(s32[128]{0:T(128)} %param.11) | copy-start | bytes 1540
  50.4 11.1 %collective-permute-start = (bf16[1,2,2048,16]{2,3,1,0:T(8,128)(2,1)S(1)}, bf16[1,2,2048,16]{2,3,1,0:T(8,128)(2,1)S(1)}, u32[]{:S(2)}, u32[]{:S(2)}) collective-permute-start(bf16[1,2,2048,16]{2,3,1,0:T(8,128)(2,1)S(1)} %copy.61), channel_id=1, source_target_pairs={{0,1},{1,2},{2,3},{3,4},{4,5},{5,6},{6,7},{7,8},{8,9},{9,10},{10,1... | collective-permute-start | bytes 393224 | tf_op jit(solution)/shard_map/ppermute | solution.py:20
  55.3 8.8 %copy-start.4 = (bf16[4096,128]{1,0:T(8,128)(2,1)S(1)}, bf16[4096,128]{1,0:T(8,128)(2,1)}, u32[]{:S(2)}) copy-start(bf16[4096,128]{1,0:T(8,128)(2,1)} %copy-done.3) | copy-start | bytes 3145732
  55.3 7.5 %collective-permute-start.1 = (bf16[1,2,2048,16]{2,3,1,0:T(8,128)(2,1)S(1)}, bf16[1,2,2048,16]{2,3,1,0:T(8,128)(2,1)S(1)}, u32[]{:S(2)}, u32[]{:S(2)}) collective-permute-start(bf16[1,2,2048,16]{2,3,1,0:T(8,128)(2,1)S(1)} %copy.63), channel_id=1, source_target_pairs={{1,0},{2,1},{3,2},{4,3},{5,4},{6,5},{7,6},{8,7},{9,8},{10,9},{11,1... | collective-permute-start | bytes 393224 | tf_op jit(solution)/shard_map/ppermute | solution.py:22
  59.0 5.2 %copy-start.8 = (f32[1,2048]{1,0:T(1,128)S(1)}, f32[1,2048]{1,0:T(1,128)}, u32[]{:S(2)}) copy-start(f32[1,2048]{1,0:T(1,128)} %get-tuple-element.26) | copy-start | bytes 24580
  59.0 5.2 %copy-start.9 = (f32[1,2048]{1,0:T(1,128)S(1)}, f32[1,2048]{1,0:T(1,128)}, u32[]{:S(2)}) copy-start(f32[1,2048]{1,0:T(1,128)} %get-tuple-element.27) | copy-start | bytes 24580
  59.0 5.2 %copy-start.10 = (f32[1,2048]{1,0:T(1,128)S(1)}, f32[1,2048]{1,0:T(1,128)}, u32[]{:S(2)}) copy-start(f32[1,2048]{1,0:T(1,128)} %get-tuple-element.28) | copy-start | bytes 24580
  59.1 5.2 %copy-start.11 = (f32[1,2048]{1,0:T(1,128)S(1)}, f32[1,2048]{1,0:T(1,128)}, u32[]{:S(2)}) copy-start(f32[1,2048]{1,0:T(1,128)} %get-tuple-element.29) | copy-start | bytes 24580
  59.1 5.2 %copy-start.12 = (f32[1,2048]{1,0:T(1,128)S(1)}, f32[1,2048]{1,0:T(1,128)}, u32[]{:S(2)}) copy-start(f32[1,2048]{1,0:T(1,128)} %get-tuple-element.30) | copy-start | bytes 24580
  59.1 5.2 %copy-start.13 = (f32[1,2048]{1,0:T(1,128)S(1)}, f32[1,2048]{1,0:T(1,128)}, u32[]{:S(2)}) copy-start(f32[1,2048]{1,0:T(1,128)} %get-tuple-element.31) | copy-start | bytes 24580
  59.1 5.2 %copy-start.14 = (f32[1,2048]{1,0:T(1,128)S(1)}, f32[1,2048]{1,0:T(1,128)}, u32[]{:S(2)}) copy-start(f32[1,2048]{1,0:T(1,128)} %get-tuple-element.32) | copy-start | bytes 24580
  59.1 5.2 %copy-start.15 = (f32[1,2048]{1,0:T(1,128)S(1)}, f32[1,2048]{1,0:T(1,128)}, u32[]{:S(2)}) copy-start(f32[1,2048]{1,0:T(1,128)} %get-tuple-element.33) | copy-start | bytes 24580
  59.1 0.6 copy-start.17
  59.1 0.6 copy-start.19
  107.6 0.7 copy-start.16
  108.8 20.7 %copy-start.20 = (s32[512,1]{0,1:T(1,128)S(1)}, s32[512,1]{0,1:T(1,128)}, u32[]{:S(2)}) copy-start(s32[512,1]{0,1:T(1,128)} %copy-done.19) | copy-start | bytes 6148
  108.8 20.7 %copy-start.18 = (s32[512,1]{0,1:T(1,128)S(1)}, s32[512,1]{0,1:T(1,128)}, u32[]{:S(2)}) copy-start(s32[512,1]{0,1:T(1,128)} %copy-done.17) | copy-start | bytes 6148
  118.3 30.3 %all-to-all-start = ((bf16[1,2,2048,128]{3,1,0,2:T(2,128)(2,1)}), bf16[1,2,2048,128]{3,1,0,2:T(2,128)(2,1)S(1)}, u32[]{:S(2)}, u32[]{:S(2)}) async-start(bf16[1,2,2048,128]{3,1,0,2:T(2,128)(2,1)} %copy.67), calls=%async_computation | async-start | bytes 2097152 | tf_op jit(solution)/shard_map/all_to_all | solution.py:109
  161.4 3.4 %copy-start.2 = (bf16[1,2,16,512,128]{4,2,3,1,0:T(8,128)(2,1)S(1)}, bf16[1,2,16,512,128]{4,2,3,1,0:T(8,128)(2,1)}, u32[]{:S(2)}) copy-start(bf16[1,2,16,512,128]{4,2,3,1,0:T(8,128)(2,1)} %bitcast_select_fusion) | copy-start | bytes 12582916
  161.4 3.5 %copy-start.6 = (f32[16,512]{0,1:T(8,128)S(1)}, f32[16,512]{0,1:T(8,128)}, u32[]{:S(2)}) copy-start(f32[16,512]{0,1:T(8,128)} %copy.75) | copy-start | bytes 98308
  171.7 5.9 %copy-start.23 = (s32[4]{0:T(128)S(1)}, s32[4]{0:T(128)}, u32[]{:S(2)}) copy-start(s32[4]{0:T(128)} %param.10) | copy-start | bytes 52
  171.7 58.5 %all-to-all-start.1 = ((bf16[2,16,512,128]{3,1,0,2:T(8,128)(2,1)}), bf16[2,16,512,128]{3,1,0,2:T(8,128)(2,1)}, u32[]{:S(2)}, u32[]{:S(2)}) async-start(bf16[2,16,512,128]{3,1,0,2:T(8,128)(2,1)} %copy.76), calls=%async_computation.1 | async-start | bytes 8388608 | tf_op jit(solution)/shard_map/all_to_all | solution.py:142
  230.2 3.1 %copy-start.5 = (bf16[1,2048,512]{2,1,0:T(8,128)(2,1)S(1)}, bf16[1,2048,512]{2,1,0:T(8,128)(2,1)}, u32[]{:S(2)}) copy-start(bf16[1,2048,512]{2,1,0:T(8,128)(2,1)} %get-tuple-element.54) | copy-start | bytes 6291460
  233.3 3.4 %copy-start.1 = (bf16[128,1,4096]{2,0,1:T(8,128)(2,1)S(1)}, bf16[128,1,4096]{2,0,1:T(8,128)(2,1)}, u32[]{:S(2)}) copy-start(bf16[128,1,4096]{2,0,1:T(8,128)(2,1)} %param.7) | copy-start | bytes 3145732
where the time goes:
time: 237 us
  other arithmetic  101 us (43%)
  waiting for transfers between devices  53.4 us (23%)
  local copies, waits for them, and re-layouts  31.9 us (13%)
  matrix products  26.3 us (11%)
  starting transfers between devices  23.9 us (10%)
    add x1, other arithmetic, whiten(): filtered + fan_taps[offset][None, None, :, None] * padded[:, :, :, offset...  40 us
    all_to_all x1, waiting for transfers between devices, body(): lax.all_to_all(cross_spec, ('group', 'shard'), split_axis=2, concat_axis=...  34.5 us
    dot_general x1, matrix products, body(): jnp.einsum('cst,tk->skc', samples, forward, preferred_element_type=jnp.fl...  22.9 us
    sub x1, other arithmetic, forward_tables(): cosine = (cos_a * cos_b - sin_a * sin_b).reshape(length, bin_count)  22 us
    another operation x4, other arithmetic  20.1 us
    all_to_all x1, waiting for transfers between devices, body(): lax.all_to_all(whitened, ('group', 'shard'), split_axis=2, concat_axis=3,...  19 us
    all_to_all x1, starting transfers between devices, body(): lax.all_to_all(whitened, ('group', 'shard'), split_axis=2, concat_axis=3,...  11.2 us
    convert_element_type x1, local copies, waits for them, and re-layouts, whiten(): (filtered * lax.rsqrt(mean_power + EPSILON)[:, None]).astype(jnp.bfloat16)  9.46 us
  transfers between devices with their start and end apart: 4, of which 2 were waited for; matrix products, arithmetic and copies ran while one was open for 10% of the time, Pallas kernels for 0%

commit v1 on v0

--- a/solution.py
+++ b/solution.py
@@ -106,7 +106,15 @@
         HALF,
     )
     whitened = whiten(padded, fan_taps)
-    banded = lax.all_to_all(whitened, ("group", "shard"), split_axis=2, concat_axis=3, tiled=True)
+    banded = jnp.concatenate(
+        lax.all_to_all(
+            jnp.stack(jnp.split(whitened, lax.axis_size(("group", "shard")), axis=2)),
+            ("group", "shard"),
+            0,
+            0,
+        ),
+        axis=3,
+    )
     first_block = pair_blocks[:, 0]
     second_block = pair_blocks[:, 1]
     blocks = banded.reshape(segments, 2, bins_device, devices, block_width)

time: 237 us -> 305 us (1.29)
  local copies, waits for them, and re-layouts: 31.9 us -> 99.2 us
    unnamed x48 -> x175, local copies, waits for them, and re-layouts: 1.42 us -> 77.6 us
    convert_element_type x1 -> x0, local copies, waits for them, and re-layouts: 9.46 us -> none  [whiten(): (filtered * lax.rsqrt(mean_power + EPSILON)[:, None]).astype(jnp.bfloat16)]
  transfers between devices with their start and end apart: 4 -> 4, of which waited for: 2 -> 2; matrix products, arithmetic and copies ran while one was open for 10% -> 8% of each run, Pallas kernels for 0% -> 0%
where the time goes in v1:
time: 305 us; the launch traced here: 304 us
  other arithmetic  101 us (33%)
  local copies, waits for them, and re-layouts  99.2 us (33%)
  waiting for transfers between devices  53.4 us (18%)
  matrix products  26.3 us (9%)
  starting transfers between devices  23.9 us (8%)
    unnamed x175, local copies, waits for them, and re-layouts  77.6 us
    add x1, other arithmetic, whiten(): filtered + fan_taps[offset][None, None, :, None] * padded[:, :, :, offset...  40 us
    all_to_all x1, waiting for transfers between devices, body(): lax.all_to_all(cross_spec, ('group', 'shard'), split_axis=2, concat_axis=...  34.5 us
    dot_general x1, matrix products, body(): jnp.einsum('cst,tk->skc', samples, forward, preferred_element_type=jnp.fl...  22.9 us
    sub x1, other arithmetic, forward_tables(): cosine = (cos_a * cos_b - sin_a * sin_b).reshape(length, bin_count)  22 us
    another operation x4, other arithmetic  20.1 us
    all_to_all x1, waiting for transfers between devices, body(): lax.all_to_all(jnp.stack(jnp.split(whitened, lax.axis_size(('group', 'sha...  19 us
    all_to_all x1, starting transfers between devices, body(): lax.all_to_all(jnp.stack(jnp.split(whitened, lax.axis_size(('group', 'sha...  11.2 us
  transfers between devices with their start and end apart: 4, of which 2 were waited for; matrix products, arithmetic and copies ran while one was open for 8% of the time, Pallas kernels for 0%

profile of v1, /device:TPU:1, one launch (start us, length us, event | category | flops | bytes accessed | tf_op | source)
XLA Modules:
  0.0 304.1 jit_solution(13316119830047584969)
XLA Ops:
  0.0 2.0 fusion.74
  2.1 2.1 fusion.77
  4.2 22.0 %multiply_subtract_fusion = (f32[64,64,2048]{2,1,0:T(8,128)}, f32[64,64,2048]{2,1,0:T(8,128)}) fusion(f32[64,2048]{1,0:T(8,128)S(1)} %get-tuple-element.59, f32[64,2048]{1,0:T(8,128)S(1)} %get-tuple-element.58, f32[64,2048]{1,0:T(8,128)S(1)} %get-tuple-element.60, f32[64,2048]{1,0:T(8,128)S(1)} %get-tuple-element.57), kind=kLoop, calls=%fused_computation.5 | loop fusion | flops 58720256 | bytes 69206016 | tf_op jit(solution)/shard_map/sub | solution.py:40
  26.2 22.9 %fusion.3 = bf16[4096,128]{1,0:T(8,128)(2,1)S(1)} fusion(f32[4096,2048]{1,0:T(8,128)} %bitcast.668, f32[4096,2048]{1,0:T(8,128)} %bitcast.667, bf16[128,1,4096]{2,0,1:T(8,128)(2,1)S(1)} %copy-done), kind=kOutput, calls=%fused_computation.76 | convolution fusion | flops 4345823232 | bytes 69206016 | tf_op jit(solution)/shard_map/cst,tk->skc/dot_general | solution.py:102
  50.4 4.6 %collective-permute-start = (bf16[1,2,2048,16]{2,3,1,0:T(8,128)(2,1)S(1)}, bf16[1,2,2048,16]{2,3,1,0:T(8,128)(2,1)S(1)}, u32[]{:S(2)}, u32[]{:S(2)}) collective-permute-start(bf16[1,2,2048,16]{2,3,1,0:T(8,128)(2,1)S(1)} %copy.328), channel_id=1, source_target_pairs={{0,1},{1,2},{2,3},{3,4},{4,5},{5,6},{6,7},{7,8},{8,9},{9,10},{10,1... | collective-permute-start | bytes 393224 | tf_op jit(solution)/shard_map/ppermute | solution.py:20
  55.3 2.2 collective-permute-start.1
  57.6 0.7 fusion.93
  58.3 0.7 fusion.94
  60.1 0.9 copy.341
  60.9 0.6 fusion.86
  61.5 1.3 copy.329
  62.9 1.3 copy.331
  64.3 40.0 %multiply_add_fusion = f32[1,2,2048,128]{3,2,1,0:T(8,128)S(1)} fusion(bf16[1,2,2048,128]{3,2,1,0:T(8,128)(2,1)S(1)} %bitcast.670, bf16[1,2,2048,16]{3,2,1,0:T(8,128)(2,1)} %copy.331, bf16[1,2,2048,16]{3,2,1,0:T(8,128)(2,1)} %copy.329, f32[2048]{0:T(1024)} %bitcast.707, f32[2048]{0:T(1024)} %bitcast.708, f32[2048]{0:T(1024)S(1)} %bitcast.677, ...), kind=kLoop, calls=%fused_computation.103 | loop fusion | flops 101711872 | bytes 3678208 | tf_op jit(solution)/shard_map/add | solution.py:84
  104.3 0.6 fusion.60
  105.0 1.3 copy.333
  106.3 1.3 bitcast_add_fusion
  108.9 0.6 constant_dynamic-update-slice_fusion.127
  109.5 0.6 constant_dynamic-update-slice_fusion.126
  110.1 0.6 constant_dynamic-update-slice_fusion.125
  185.7 11.2 %all-to-all-start = ((bf16[128,1,2,16,128]{4,3,2,1,0:T(8,128)(2,1)}), bf16[128,1,2,16,128]{4,3,2,1,0:T(8,128)(2,1)S(1)}, u32[]{:S(2)}, u32[]{:S(2)}) async-start(bf16[128,1,2,16,128]{4,3,2,1,0:T(8,128)(2,1)} %constant_dynamic-update-slice_fusion), calls=%async_computation | async-start | bytes 2097152 | tf_op jit(solution)/shard_map/all_to_all | solution.py:110
  197.0 19.0 %all-to-all-done = bf16[128,1,2,16,128]{4,3,2,1,0:T(8,128)(2,1)S(1)} async-done(((bf16[128,1,2,16,128]{4,3,2,1,0:T(8,128)(2,1)}), bf16[128,1,2,16,128]{4,3,2,1,0:T(8,128)(2,1)S(1)}, u32[]{:S(2)}, u32[]{:S(2)}) %all-to-all-start) | async-done | bytes 1048608 | tf_op jit(solution)/shard_map/all_to_all | solution.py:110
  217.3 3.5 %gather_fusion.1 = bf16[512,2,16,128]{3,2,1,0:T(8,128)(2,1)} fusion(bf16[2,16,128,128]{3,1,2,0:T(8,128)(2,1)S(1)} %maximum_bitcast_fusion.6, s32[1024]{0:T(1024)S(1)} %pad_clamp_fusion), kind=kCustom, calls=%fused_computation.1.clone | custom fusion | bytes 8390656 | tf_op jit(solution)/shard_map/jit(_take)/gather | solution.py:123
  220.8 4.6 %bitcast_select_fusion = bf16[1,2,16,512,128]{4,2,3,1,0:T(8,128)(2,1)} fusion(bf16[512,2,16,128]{3,2,1,0:T(8,128)(2,1)} %gather_fusion.1, pred[512]{0:T(512)(128)(4,1)S(1)} %compare_and_fusion), kind=kLoop, calls=%fused_computation.90 | loop fusion | flops 2097152 | bytes 8389120 | tf_op jit(solution)/shard_map/jit(_take)/select_n | solution.py:123
  225.3 3.5 %gather_fusion = bf16[512,2,16,128]{3,2,1,0:T(8,128)(2,1)} fusion(bf16[2,16,128,128]{3,1,2,0:T(8,128)(2,1)S(1)} %bitcast.666, s32[1024]{0:T(1024)S(1)} %pad_clamp_fusion.1), kind=kCustom, calls=%fused_computation.clone | custom fusion | bytes 8390656 | tf_op jit(solution)/shard_map/jit(_take)/gather | solution.py:122
  228.9 3.4 %bitcast_select_fusion.1 = bf16[1,2,16,512,128]{4,2,1,3,0:T(8,128)(2,1)S(1)} fusion(bf16[512,2,16,128]{3,2,1,0:T(8,128)(2,1)} %gather_fusion, pred[512]{0:T(512)(128)(4,1)S(1)} %compare_and_fusion.1), kind=kLoop, calls=%fused_computation.91 | loop fusion | flops 2097152 | bytes 8389120 | tf_op jit(solution)/shard_map/jit(_take)/select_n | solution.py:122
  232.3 3.6 %fusion.20 = (bf16[1,16,512,128]{3,1,2,0:T(8,128)(2,1)S(1)}, bf16[1,16,512,128]{3,1,2,0:T(8,128)(2,1)S(1)}) fusion(f32[16,512]{0,1:T(8,128)S(1)} %copy-done.6, f32[16,512]{0,1:T(8,128)S(1)} %copy.338, bf16[1,2,16,512,128]{4,2,3,1,0:T(8,128)(2,1)S(1)} %copy-done.2, bf16[1,2,16,512,128]{4,2,1,3,0:T(8,128)(2,1)S(1)} %bitcast_select_fusion.1), kind=kLoop, calls=%fused_computation.99 | loop fusion | flops 18874368 | bytes 12648448 | tf_op jit(solution)/shard_map/stack | solution.py:147
  236.3 2.7 copy.342
  239.1 5.8 %all-to-all-start.1 = ((bf16[2,16,512,128]{3,1,0,2:T(8,128)(2,1)}), bf16[2,16,512,128]{3,1,0,2:T(8,128)(2,1)}, u32[]{:S(2)}, u32[]{:S(2)}) async-start(bf16[2,16,512,128]{3,1,0,2:T(8,128)(2,1)} %copy.342), calls=%async_computation.1 | async-start | bytes 8388608 | tf_op jit(solution)/shard_map/all_to_all | solution.py:150
  245.0 18.2 %cosine_convert_fusion = (bf16[1,2048,512]{2,1,0:T(8,128)(2,1)S(1)}, bf16[1,2048,512]{2,1,0:T(8,128)(2,1)}) fusion(s32[512]{0:T(512)S(1)} %iota_add_fusion.2), kind=kLoop, calls=%fused_computation.93 | loop fusion | flops 17825792 | bytes 4196352 | tf_op jit(solution)/shard_map/convert.12
  263.2 34.5 %all-to-all-done.1 = bf16[2,16,512,128]{3,1,0,2:T(8,128)(2,1)} async-done(((bf16[2,16,512,128]{3,1,0,2:T(8,128)(2,1)}), bf16[2,16,512,128]{3,1,0,2:T(8,128)(2,1)}, u32[]{:S(2)}, u32[]{:S(2)}) %all-to-all-start.1) | async-done | bytes 4194336 | tf_op jit(solution)/shard_map/all_to_all | solution.py:150
  297.6 3.1 %copy.344 = bf16[2,128,16,4,128]{4,2,1,3,0:T(8,128)(2,1)S(1)} copy(bf16[2,128,16,4,128]{4,2,0,3,1:T(8,128)(2,1)} %bitcast.193) | data formatting | bytes 8388608 | tf_op jit(solution)/shard_map/all_to_all | solution.py:150
  300.8 3.3 %fusion.23 = f32[4,128,512]{2,1,0:T(8,128)} fusion(bf16[2,2048,4,128]{3,1,2,0:T(8,128)(2,1)S(1)} %bitcast.675, bf16[1,2048,512]{2,1,0:T(8,128)(2,1)S(1)} %copy-done.5, bf16[1,2048,512]{2,1,0:T(8,128)(2,1)S(1)} %get-tuple-element.55, f32[4]{0:T(128)S(1)} %convert_multiply_fusion.4), kind=kOutput, calls=%fused_computation.105 | convolution fusion | flops 2149842944 | bytes 9437200 | tf_op jit(solution)/shard_map/rkpc,rkl->pcl/dot_general | solution.py:154
  (207 shorter events, 80.6 us)
Async XLA Ops:
  0.0 26.2 %copy-start = (bf16[128,1,4096]{2,0,1:T(8,128)(2,1)S(1)}, bf16[128,1,4096]{2,0,1:T(8,128)(2,1)}, u32[]{:S(2)}) copy-start(bf16[128,1,4096]{2,0,1:T(8,128)(2,1)} %param.7) | copy-start | bytes 3145732
  49.1 1.0 copy-start.3
  50.1 7.5 %copy-start.7 = (f32[33,2048]{1,0:T(8,128)S(1)}, f32[33,2048]{1,0:T(8,128)}, u32[]{:S(2)}) copy-start(f32[33,2048]{1,0:T(8,128)} %param.8) | copy-start | bytes 811012
  50.1 9.0 %copy-start.21 = (s32[512,2]{0,1:T(2,128)S(1)}, s32[512,2]{0,1:T(2,128)}, u32[]{:S(2)}) copy-start(s32[512,2]{0,1:T(2,128)} %param.9) | copy-start | bytes 12292
  50.1 9.0 %copy-start.22 = (s32[128]{0:T(128)S(1)}, s32[128]{0:T(128)}, u32[]{:S(2)}) copy-start(s32[128]{0:T(128)} %param.11) | copy-start | bytes 1540
  50.4 11.1 %collective-permute-start = (bf16[1,2,2048,16]{2,3,1,0:T(8,128)(2,1)S(1)}, bf16[1,2,2048,16]{2,3,1,0:T(8,128)(2,1)S(1)}, u32[]{:S(2)}, u32[]{:S(2)}) collective-permute-start(bf16[1,2,2048,16]{2,3,1,0:T(8,128)(2,1)S(1)} %copy.328), channel_id=1, source_target_pairs={{0,1},{1,2},{2,3},{3,4},{4,5},{5,6},{6,7},{7,8},{8,9},{9,10},{10,1... | collective-permute-start | bytes 393224 | tf_op jit(solution)/shard_map/ppermute | solution.py:20
  55.3 8.8 %copy-start.4 = (bf16[4096,128]{1,0:T(8,128)(2,1)S(1)}, bf16[4096,128]{1,0:T(8,128)(2,1)}, u32[]{:S(2)}) copy-start(bf16[4096,128]{1,0:T(8,128)(2,1)} %copy-done.3) | copy-start | bytes 3145732
  55.3 7.5 %collective-permute-start.1 = (bf16[1,2,2048,16]{2,3,1,0:T(8,128)(2,1)S(1)}, bf16[1,2,2048,16]{2,3,1,0:T(8,128)(2,1)S(1)}, u32[]{:S(2)}, u32[]{:S(2)}) collective-permute-start(bf16[1,2,2048,16]{2,3,1,0:T(8,128)(2,1)S(1)} %copy.330), channel_id=1, source_target_pairs={{1,0},{2,1},{3,2},{4,3},{5,4},{6,5},{7,6},{8,7},{9,8},{10,9},{11,1... | collective-permute-start | bytes 393224 | tf_op jit(solution)/shard_map/ppermute | solution.py:22
  59.0 5.2 %copy-start.8 = (f32[1,2048]{1,0:T(1,128)S(1)}, f32[1,2048]{1,0:T(1,128)}, u32[]{:S(2)}) copy-start(f32[1,2048]{1,0:T(1,128)} %get-tuple-element.28) | copy-start | bytes 24580
  59.0 5.2 %copy-start.9 = (f32[1,2048]{1,0:T(1,128)S(1)}, f32[1,2048]{1,0:T(1,128)}, u32[]{:S(2)}) copy-start(f32[1,2048]{1,0:T(1,128)} %get-tuple-element.29) | copy-start | bytes 24580
  59.0 5.2 %copy-start.10 = (f32[1,2048]{1,0:T(1,128)S(1)}, f32[1,2048]{1,0:T(1,128)}, u32[]{:S(2)}) copy-start(f32[1,2048]{1,0:T(1,128)} %get-tuple-element.30) | copy-start | bytes 24580
  59.1 5.2 %copy-start.11 = (f32[1,2048]{1,0:T(1,128)S(1)}, f32[1,2048]{1,0:T(1,128)}, u32[]{:S(2)}) copy-start(f32[1,2048]{1,0:T(1,128)} %get-tuple-element.31) | copy-start | bytes 24580
  59.1 5.2 %copy-start.12 = (f32[1,2048]{1,0:T(1,128)S(1)}, f32[1,2048]{1,0:T(1,128)}, u32[]{:S(2)}) copy-start(f32[1,2048]{1,0:T(1,128)} %get-tuple-element.32) | copy-start | bytes 24580
  59.1 5.2 %copy-start.13 = (f32[1,2048]{1,0:T(1,128)S(1)}, f32[1,2048]{1,0:T(1,128)}, u32[]{:S(2)}) copy-start(f32[1,2048]{1,0:T(1,128)} %get-tuple-element.33) | copy-start | bytes 24580
  59.1 5.2 %copy-start.14 = (f32[1,2048]{1,0:T(1,128)S(1)}, f32[1,2048]{1,0:T(1,128)}, u32[]{:S(2)}) copy-start(f32[1,2048]{1,0:T(1,128)} %get-tuple-element.34) | copy-start | bytes 24580
  59.1 5.2 %copy-start.15 = (f32[1,2048]{1,0:T(1,128)S(1)}, f32[1,2048]{1,0:T(1,128)}, u32[]{:S(2)}) copy-start(f32[1,2048]{1,0:T(1,128)} %get-tuple-element.35) | copy-start | bytes 24580
  59.1 0.6 copy-start.17
  59.1 0.6 copy-start.19
  107.6 0.7 copy-start.16
  108.9 88.0 %copy-start.20 = (s32[512,1]{0,1:T(1,128)S(1)}, s32[512,1]{0,1:T(1,128)}, u32[]{:S(2)}) copy-start(s32[512,1]{0,1:T(1,128)} %copy-done.19) | copy-start | bytes 6148
  109.5 87.5 %copy-start.18 = (s32[512,1]{0,1:T(1,128)S(1)}, s32[512,1]{0,1:T(1,128)}, u32[]{:S(2)}) copy-start(s32[512,1]{0,1:T(1,128)} %copy-done.17) | copy-start | bytes 6148
  185.7 30.3 %all-to-all-start = ((bf16[128,1,2,16,128]{4,3,2,1,0:T(8,128)(2,1)}), bf16[128,1,2,16,128]{4,3,2,1,0:T(8,128)(2,1)S(1)}, u32[]{:S(2)}, u32[]{:S(2)}) async-start(bf16[128,1,2,16,128]{4,3,2,1,0:T(8,128)(2,1)} %constant_dynamic-update-slice_fusion), calls=%async_computation | async-start | bytes 2097152 | tf_op jit(solution)/shard_map/all_to_all | solution.py:110
  228.9 3.4 %copy-start.2 = (bf16[1,2,16,512,128]{4,2,3,1,0:T(8,128)(2,1)S(1)}, bf16[1,2,16,512,128]{4,2,3,1,0:T(8,128)(2,1)}, u32[]{:S(2)}) copy-start(bf16[1,2,16,512,128]{4,2,3,1,0:T(8,128)(2,1)} %bitcast_select_fusion) | copy-start | bytes 12582916
  228.9 3.5 %copy-start.6 = (f32[16,512]{0,1:T(8,128)S(1)}, f32[16,512]{0,1:T(8,128)}, u32[]{:S(2)}) copy-start(f32[16,512]{0,1:T(8,128)} %copy.341) | copy-start | bytes 98308
  239.1 5.9 %copy-start.23 = (s32[4]{0:T(128)S(1)}, s32[4]{0:T(128)}, u32[]{:S(2)}) copy-start(s32[4]{0:T(128)} %param.10) | copy-start | bytes 52
  239.1 58.5 %all-to-all-start.1 = ((bf16[2,16,512,128]{3,1,0,2:T(8,128)(2,1)}), bf16[2,16,512,128]{3,1,0,2:T(8,128)(2,1)}, u32[]{:S(2)}, u32[]{:S(2)}) async-start(bf16[2,16,512,128]{3,1,0,2:T(8,128)(2,1)} %copy.342), calls=%async_computation.1 | async-start | bytes 8388608 | tf_op jit(solution)/shard_map/all_to_all | solution.py:150
  297.6 3.1 %copy-start.5 = (bf16[1,2048,512]{2,1,0:T(8,128)(2,1)S(1)}, bf16[1,2048,512]{2,1,0:T(8,128)(2,1)}, u32[]{:S(2)}) copy-start(bf16[1,2048,512]{2,1,0:T(8,128)(2,1)} %get-tuple-element.56) | copy-start | bytes 6291460
  300.7 3.4 %copy-start.1 = (bf16[128,1,4096]{2,0,1:T(8,128)(2,1)S(1)}, bf16[128,1,4096]{2,0,1:T(8,128)(2,1)}, u32[]{:S(2)}) copy-start(bf16[128,1,4096]{2,0,1:T(8,128)(2,1)} %param.7) | copy-start | bytes 3145732
